TPU v7x, 32 devices: a whole 2x2x4 slice. The times are simulated.
32 devices in a mesh: stream: 4 (over y, core), azim: 8 (over z, x).
Axes of the slice: x: 2, y: 2, z: 4, core: 2. Of those that a mesh axis runs over, the one named last changes fastest.
Arguments:
- fluid: float32 [4, 256, 256, 128], P(None, 'stream', 'azim'), may hold values from -4 to 4
- bubbles: float32 [16384, 5, 128], P(('stream', 'azim'))
- counts: int32 [32], P(('stream', 'azim')), may hold values from 128 to 512
- outgoing_block_order: int32 [16384], P(('stream', 'azim')), may hold values from 0 to 511, as said below
- tiles_first_update: int32 [16384], P(('stream', 'azim')), may hold values from 0 to 2047
- tiles_after: int32 [16384], P(('stream', 'azim')), may hold values from 0 to 2047
Outputs:
- fluid_out: float32 [4, 256, 256, 128], P(None, 'stream', 'azim')
- bubbles_out: float32 [16384, 5, 128], P(('stream', 'azim'))
- void_fraction: float32 [256, 256, 128], P('stream', 'azim')
Inputs may be any that keep to these rules, and one draw needn't show every extreme that they name: `outgoing_block_order`: for each device, its 512 entries are each of 0 to 511 once.
All inputs are finite; a program needn't handle non-finite values.
Results may differ from a plain program's by a relative error of at most 0.000076.
Values sent between devices are 32-bit elements; how exact they have to be, the bound alone decides.
A program may use at most 128 MiB of HBM per device.

v0:
```python
import jax
import jax.numpy as jnp
from jax import lax
from jax.sharding import PartitionSpec as P

SUBSTEPS = 8


TIME_STEP = 0.25
MEAN_FLOW = 0.5
DIFFUSION = 0.1
KERNEL_WIDTH = 1.5
GAS_INDEX = 4.2
PRESSURE_COUPLING = 0.3
AMBIENT = 1.0
RELAX_TIME = 0.5
VISCOUS = 0.08
SOURCE_GAIN = 0.05
VOID_SCALE = 0.01
FOUR_PI = 12.566370614359172


def with_halo(cells, sides, width, closed):
    for axis, dim in sides:
        count = lax.axis_size(axis)
        ends = count if closed else count - 1
        head = lax.slice_in_dim(cells, 0, width, axis=dim)
        tail = lax.slice_in_dim(cells, cells.shape[dim] - width, cells.shape[dim], axis=dim)
        cells = jnp.concatenate(
            [
                lax.ppermute(tail, axis, [(i, (i + 1) % count) for i in range(ends)]),
                cells,
                lax.ppermute(head, axis, [((i + 1) % count, i) for i in range(ends)]),
            ],
            axis=dim,
        )
    return cells


def kernel_weights(position, cell_centres):
    offset = (position[:, :, None] - cell_centres) / KERNEL_WIDTH
    raw = jnp.exp(-0.5 * offset * offset)
    return raw / jnp.sum(raw, axis=-1, keepdims=True)


def advance_group(packed_blocks):
    bubble_state, tile_row_count, alive_flags = packed_blocks
    cell_centres = jnp.arange(tile_row_count.shape[-1], dtype=jnp.int32).astype(jnp.float32)
    weights = kernel_weights(bubble_state[:, 2], cell_centres)
    sampled = jnp.einsum("gbk,gck->gcb", weights, tile_row_count, precision=lax.Precision.HIGHEST)
    pressure = sampled[:, 0]
    velocity = sampled[:, 1]
    radius = bubble_state[:, 0]
    growth = bubble_state[:, 1]
    position = bubble_state[:, 2]
    bubble_speed = bubble_state[:, 3]
    rest_radius = bubble_state[:, 4]
    substep_size = TIME_STEP / SUBSTEPS
    for substep in range(SUBSTEPS):
        gas = jnp.exp(GAS_INDEX * jnp.log(rest_radius / radius))
        accel = (
            gas
            - AMBIENT
            - PRESSURE_COUPLING * pressure
            - 1.5 * growth * growth
            - VISCOUS * growth / radius
        ) / radius
        growth = growth + substep_size * accel
        radius = radius + substep_size * growth
        bubble_speed = bubble_speed + substep_size * (velocity - bubble_speed) / RELAX_TIME
        position = position + substep_size * bubble_speed
    new_state = jnp.stack([radius, growth, position, bubble_speed, rest_radius], axis=1)
    weights = kernel_weights(position, cell_centres)
    source_amounts = jnp.stack(
        [
            SOURCE_GAIN * FOUR_PI * radius * radius * growth,
            VOID_SCALE * FOUR_PI / 3.0 * radius * radius * radius,
        ],
        axis=1,
    )
    source_amounts = source_amounts * alive_flags[:, None, None]
    spread_sources = jnp.einsum(
        "gbk,gcb->gck", weights, source_amounts, precision=lax.Precision.HIGHEST
    )
    return (new_state, spread_sources)


def advance_every_group(bubble_state, tile_row_count, alive_flags):
    bubble_groups = bubble_state.shape[0] // 64
    new_state, spread_sources = lax.map(
        advance_group,
        (
            bubble_state.reshape((bubble_groups, 64) + bubble_state.shape[1:]),
            tile_row_count.reshape((bubble_groups, 64) + tile_row_count.shape[1:]),
            alive_flags.reshape(bubble_groups, 64),
        ),
    )
    return (new_state.reshape(bubble_state.shape), spread_sources.reshape(tile_row_count.shape))


def fluid_update(
    flow_field, stream_up, stream_down, azim_up, azim_down, radial_up, radial_down, source
):
    d_stream = 0.5 * (stream_up - stream_down)
    d_azim = 0.5 * (azim_up - azim_down)
    d_radial = 0.5 * (radial_up - radial_down)
    pressure_rate = -MEAN_FLOW * d_stream[0] - d_stream[1] - d_azim[2] - d_radial[3] - source
    stream_rate = -MEAN_FLOW * d_stream[1] - d_stream[0]
    azim_rate = -MEAN_FLOW * d_stream[2] - d_azim[0]
    radial_rate = -MEAN_FLOW * d_stream[3] - d_radial[0]
    change = jnp.stack([pressure_rate, stream_rate, azim_rate, radial_rate])
    laplace = (
        stream_up + stream_down + azim_up + azim_down + radial_up + radial_down - 6.0 * flow_field
    )
    return flow_field + TIME_STEP * change + DIFFUSION * laplace


def fluid_step(flow_field, source):
    stream_pad = with_halo(flow_field, (("stream", 1),), 1, False)
    azim_pad = with_halo(flow_field, (("azim", 2),), 1, True)
    radial_pad = jnp.pad(flow_field, ((0, 0), (0, 0), (0, 0), (1, 1)))
    return fluid_update(
        flow_field,
        stream_pad[:, 2:],
        stream_pad[:, :-2],
        azim_pad[:, :, 2:],
        azim_pad[:, :, :-2],
        radial_pad[..., 2:],
        radial_pad[..., :-2],
        source,
    )


def local_update(flow_field, bubble_state, tile_indices, alive_flags):
    selected = jnp.stack([flow_field[0], flow_field[3]]).reshape(2, -1, flow_field.shape[-1])
    tile_row_count = jnp.take(selected, tile_indices, axis=1).transpose(1, 0, 2)
    bubble_state, spread_sources = advance_every_group(bubble_state, tile_row_count, alive_flags)
    grid = jnp.zeros_like(selected).at[:, tile_indices].add(spread_sources.transpose(1, 0, 2))
    grid = grid.reshape((2,) + flow_field.shape[1:])
    return (fluid_step(flow_field, grid[0]), bubble_state, grid[1])


def on_device(fluid, bubbles, counts, outgoing_block_order, tiles_first_update, tiles_after):
    alive_flags = (jnp.arange(bubbles.shape[0], dtype=jnp.int32) < counts[0]).astype(jnp.float32)
    flow_field, bubble_state, void_before_update = local_update(
        fluid, bubbles, tiles_first_update, alive_flags
    )
    outgoing = jnp.take(bubble_state, outgoing_block_order, axis=0)
    outgoing_alive_flags = jnp.take(alive_flags, outgoing_block_order, axis=0)
    arrived, arrived_live = (
        lax.all_to_all(outgoing, ("stream", "azim"), split_axis=0, concat_axis=0, tiled=True),
        lax.all_to_all(
            outgoing_alive_flags, ("stream", "azim"), split_axis=0, concat_axis=0, tiled=True
        ),
    )
    flow_field, bubble_state, void_field = local_update(
        flow_field, arrived, tiles_after, arrived_live
    )
    return (flow_field, bubble_state * arrived_live[:, None, None], void_field)


def solution(mesh):
    return jax.shard_map(
        on_device,
        mesh=mesh,
        in_specs=(
            P(None, "stream", "azim", None),
            P(("stream", "azim"), None, None),
            P(("stream", "azim")),
            P(("stream", "azim")),
            P(("stream", "azim")),
            P(("stream", "azim")),
        ),
        out_specs=(
            P(None, "stream", "azim", None),
            P(("stream", "azim"), None, None),
            P("stream", "azim", None),
        ),
        check_vma=False,
    )
```

profile of v0, /device:TPU:17, one launch (start us, length us, event | category | flops | bytes accessed | tf_op | source)
XLA Modules:
  0.0 517.5 jit_solution(4212522839261922217)
XLA Ops:
  0.6 4.6 copy.117
  7.7 3.1 collective-permute-start
  10.9 3.0 collective-permute-start.1
  14.6 3.5 gather_fusion.1
  18.8 8.2 %all-to-all-start.1 = ((f32[32,16,1]{1,2,0:T(1,128)}), f32[32,16,1]{1,2,0:T(1,128)S(1)}, u32[]{:S(2)}, u32[]{:S(2)}) async-start(f32[32,16,1]{1,2,0:T(1,128)} %bitcast.48), calls=%async_computation.1 | async-start | bytes 32768 | tf_op jit(solution)/shard_map/all_to_all | solution.py:152
  35.1 163.4 %while.30 = (s32[]{:T(128)}, f32[8,64,5,128]{3,1,0,2:T(8,128)S(1)}, f32[8,64,2,128]{3,2,1,0:T(2,128)S(1)}, f32[8,64,5,128]{3,1,0,2:T(8,128)}, f32[8,64,2,128]{3,...) while((s32[]{:T(128)}, f32[8,64,5,128]{3,1,0,2:T(8,128)S(1)}, f32[8,64,2,128]{3,2,1,0:T(2,128)S(1)}, ...), condition=%wide.region_3.5_spmd, body=%wide.region_0.4_spmd.sunk | while | flops 73212032 | bytes 2329953 | solution.py:90
  38.5 8.3 %fusion.208 = f32[64,2,128]{2,1,0:T(2,128)S(1)} fusion(f32[64,128]{1,0:T(8,128)S(1)} %fusion.207, f32[128]{0:T(128)S(1)} %iota_convert_fusion.4, f32[64,128]{1,0:T(8,128)S(1)} %slice_bitcast_fusion.4, f32[8,64,2,128]{3,2,1,0:T(2,128)S(1)} %get-tuple-element.507, s32[]{:T(128)} %get-tuple-element.496), kind=kOutput, calls=%fused_computation.19.clone.1 | convolution fusion | flops 30408704 | bytes 197124 | tf_op jit(solution)/shard_map/while/body/eval_jaxpr/gbk,gck->gcb/dot_general | solution.py:50
  49.7 5.7 %fusion.214 = f32[8,64,2,128]{3,2,1,0:T(2,128)S(1)} fusion(f32[8,64,2,128]{3,2,1,0:T(2,128)S(1)} %get-tuple-element.498, s32[]{:T(128)} %get-tuple-element.496, f32[64,128]{1,0:T(8,128)S(1)} %fusion.212, f32[64,128]{1,0:T(8,128)S(1)} %multiply_add_fusion.38, f32[128]{0:T(128)S(1)} %iota_convert_fusion.4, f32[64,2,128]{2,0,1:T(8,128)S(1)} %maximum_multiply_fusion.6), kind=kOutput, calls=%fused_computation.31.clone.1 | convolution fusion | flops 30408704 | bytes 197124 | tf_op jit(solution)/shard_map/while/body/eval_jaxpr/gbk,gcb->gck/dot_general | solution.py:82
  58.9 8.3 %fusion.208 = f32[64,2,128]{2,1,0:T(2,128)S(1)} fusion(f32[64,128]{1,0:T(8,128)S(1)} %fusion.207, f32[128]{0:T(128)S(1)} %iota_convert_fusion.4, f32[64,128]{1,0:T(8,128)S(1)} %slice_bitcast_fusion.4, f32[8,64,2,128]{3,2,1,0:T(2,128)S(1)} %get-tuple-element.507, s32[]{:T(128)} %get-tuple-element.496), kind=kOutput, calls=%fused_computation.19.clone.1 | convolution fusion | flops 30408704 | bytes 197124 | tf_op jit(solution)/shard_map/while/body/eval_jaxpr/gbk,gck->gcb/dot_general | solution.py:50
  70.1 5.7 %fusion.214 = f32[8,64,2,128]{3,2,1,0:T(2,128)S(1)} fusion(f32[8,64,2,128]{3,2,1,0:T(2,128)S(1)} %get-tuple-element.498, s32[]{:T(128)} %get-tuple-element.496, f32[64,128]{1,0:T(8,128)S(1)} %fusion.212, f32[64,128]{1,0:T(8,128)S(1)} %multiply_add_fusion.38, f32[128]{0:T(128)S(1)} %iota_convert_fusion.4, f32[64,2,128]{2,0,1:T(8,128)S(1)} %maximum_multiply_fusion.6), kind=kOutput, calls=%fused_computation.31.clone.1 | convolution fusion | flops 30408704 | bytes 197124 | tf_op jit(solution)/shard_map/while/body/eval_jaxpr/gbk,gcb->gck/dot_general | solution.py:82
  79.3 8.3 %fusion.208 = f32[64,2,128]{2,1,0:T(2,128)S(1)} fusion(f32[64,128]{1,0:T(8,128)S(1)} %fusion.207, f32[128]{0:T(128)S(1)} %iota_convert_fusion.4, f32[64,128]{1,0:T(8,128)S(1)} %slice_bitcast_fusion.4, f32[8,64,2,128]{3,2,1,0:T(2,128)S(1)} %get-tuple-element.507, s32[]{:T(128)} %get-tuple-element.496), kind=kOutput, calls=%fused_computation.19.clone.1 | convolution fusion | flops 30408704 | bytes 197124 | tf_op jit(solution)/shard_map/while/body/eval_jaxpr/gbk,gck->gcb/dot_general | solution.py:50
  90.5 5.7 %fusion.214 = f32[8,64,2,128]{3,2,1,0:T(2,128)S(1)} fusion(f32[8,64,2,128]{3,2,1,0:T(2,128)S(1)} %get-tuple-element.498, s32[]{:T(128)} %get-tuple-element.496, f32[64,128]{1,0:T(8,128)S(1)} %fusion.212, f32[64,128]{1,0:T(8,128)S(1)} %multiply_add_fusion.38, f32[128]{0:T(128)S(1)} %iota_convert_fusion.4, f32[64,2,128]{2,0,1:T(8,128)S(1)} %maximum_multiply_fusion.6), kind=kOutput, calls=%fused_computation.31.clone.1 | convolution fusion | flops 30408704 | bytes 197124 | tf_op jit(solution)/shard_map/while/body/eval_jaxpr/gbk,gcb->gck/dot_general | solution.py:82
  99.7 8.3 %fusion.208 = f32[64,2,128]{2,1,0:T(2,128)S(1)} fusion(f32[64,128]{1,0:T(8,128)S(1)} %fusion.207, f32[128]{0:T(128)S(1)} %iota_convert_fusion.4, f32[64,128]{1,0:T(8,128)S(1)} %slice_bitcast_fusion.4, f32[8,64,2,128]{3,2,1,0:T(2,128)S(1)} %get-tuple-element.507, s32[]{:T(128)} %get-tuple-element.496), kind=kOutput, calls=%fused_computation.19.clone.1 | convolution fusion | flops 30408704 | bytes 197124 | tf_op jit(solution)/shard_map/while/body/eval_jaxpr/gbk,gck->gcb/dot_general | solution.py:50
  111.0 5.7 %fusion.214 = f32[8,64,2,128]{3,2,1,0:T(2,128)S(1)} fusion(f32[8,64,2,128]{3,2,1,0:T(2,128)S(1)} %get-tuple-element.498, s32[]{:T(128)} %get-tuple-element.496, f32[64,128]{1,0:T(8,128)S(1)} %fusion.212, f32[64,128]{1,0:T(8,128)S(1)} %multiply_add_fusion.38, f32[128]{0:T(128)S(1)} %iota_convert_fusion.4, f32[64,2,128]{2,0,1:T(8,128)S(1)} %maximum_multiply_fusion.6), kind=kOutput, calls=%fused_computation.31.clone.1 | convolution fusion | flops 30408704 | bytes 197124 | tf_op jit(solution)/shard_map/while/body/eval_jaxpr/gbk,gcb->gck/dot_general | solution.py:82
  120.1 8.3 %fusion.208 = f32[64,2,128]{2,1,0:T(2,128)S(1)} fusion(f32[64,128]{1,0:T(8,128)S(1)} %fusion.207, f32[128]{0:T(128)S(1)} %iota_convert_fusion.4, f32[64,128]{1,0:T(8,128)S(1)} %slice_bitcast_fusion.4, f32[8,64,2,128]{3,2,1,0:T(2,128)S(1)} %get-tuple-element.507, s32[]{:T(128)} %get-tuple-element.496), kind=kOutput, calls=%fused_computation.19.clone.1 | convolution fusion | flops 30408704 | bytes 197124 | tf_op jit(solution)/shard_map/while/body/eval_jaxpr/gbk,gck->gcb/dot_general | solution.py:50
  131.4 5.7 %fusion.214 = f32[8,64,2,128]{3,2,1,0:T(2,128)S(1)} fusion(f32[8,64,2,128]{3,2,1,0:T(2,128)S(1)} %get-tuple-element.498, s32[]{:T(128)} %get-tuple-element.496, f32[64,128]{1,0:T(8,128)S(1)} %fusion.212, f32[64,128]{1,0:T(8,128)S(1)} %multiply_add_fusion.38, f32[128]{0:T(128)S(1)} %iota_convert_fusion.4, f32[64,2,128]{2,0,1:T(8,128)S(1)} %maximum_multiply_fusion.6), kind=kOutput, calls=%fused_computation.31.clone.1 | convolution fusion | flops 30408704 | bytes 197124 | tf_op jit(solution)/shard_map/while/body/eval_jaxpr/gbk,gcb->gck/dot_general | solution.py:82
  140.6 8.3 %fusion.208 = f32[64,2,128]{2,1,0:T(2,128)S(1)} fusion(f32[64,128]{1,0:T(8,128)S(1)} %fusion.207, f32[128]{0:T(128)S(1)} %iota_convert_fusion.4, f32[64,128]{1,0:T(8,128)S(1)} %slice_bitcast_fusion.4, f32[8,64,2,128]{3,2,1,0:T(2,128)S(1)} %get-tuple-element.507, s32[]{:T(128)} %get-tuple-element.496), kind=kOutput, calls=%fused_computation.19.clone.1 | convolution fusion | flops 30408704 | bytes 197124 | tf_op jit(solution)/shard_map/while/body/eval_jaxpr/gbk,gck->gcb/dot_general | solution.py:50
  151.8 5.7 %fusion.214 = f32[8,64,2,128]{3,2,1,0:T(2,128)S(1)} fusion(f32[8,64,2,128]{3,2,1,0:T(2,128)S(1)} %get-tuple-element.498, s32[]{:T(128)} %get-tuple-element.496, f32[64,128]{1,0:T(8,128)S(1)} %fusion.212, f32[64,128]{1,0:T(8,128)S(1)} %multiply_add_fusion.38, f32[128]{0:T(128)S(1)} %iota_convert_fusion.4, f32[64,2,128]{2,0,1:T(8,128)S(1)} %maximum_multiply_fusion.6), kind=kOutput, calls=%fused_computation.31.clone.1 | convolution fusion | flops 30408704 | bytes 197124 | tf_op jit(solution)/shard_map/while/body/eval_jaxpr/gbk,gcb->gck/dot_general | solution.py:82
  161.0 8.3 %fusion.208 = f32[64,2,128]{2,1,0:T(2,128)S(1)} fusion(f32[64,128]{1,0:T(8,128)S(1)} %fusion.207, f32[128]{0:T(128)S(1)} %iota_convert_fusion.4, f32[64,128]{1,0:T(8,128)S(1)} %slice_bitcast_fusion.4, f32[8,64,2,128]{3,2,1,0:T(2,128)S(1)} %get-tuple-element.507, s32[]{:T(128)} %get-tuple-element.496), kind=kOutput, calls=%fused_computation.19.clone.1 | convolution fusion | flops 30408704 | bytes 197124 | tf_op jit(solution)/shard_map/while/body/eval_jaxpr/gbk,gck->gcb/dot_general | solution.py:50
  172.2 5.7 %fusion.214 = f32[8,64,2,128]{3,2,1,0:T(2,128)S(1)} fusion(f32[8,64,2,128]{3,2,1,0:T(2,128)S(1)} %get-tuple-element.498, s32[]{:T(128)} %get-tuple-element.496, f32[64,128]{1,0:T(8,128)S(1)} %fusion.212, f32[64,128]{1,0:T(8,128)S(1)} %multiply_add_fusion.38, f32[128]{0:T(128)S(1)} %iota_convert_fusion.4, f32[64,2,128]{2,0,1:T(8,128)S(1)} %maximum_multiply_fusion.6), kind=kOutput, calls=%fused_computation.31.clone.1 | convolution fusion | flops 30408704 | bytes 197124 | tf_op jit(solution)/shard_map/while/body/eval_jaxpr/gbk,gcb->gck/dot_general | solution.py:82
  181.4 8.3 %fusion.208 = f32[64,2,128]{2,1,0:T(2,128)S(1)} fusion(f32[64,128]{1,0:T(8,128)S(1)} %fusion.207, f32[128]{0:T(128)S(1)} %iota_convert_fusion.4, f32[64,128]{1,0:T(8,128)S(1)} %slice_bitcast_fusion.4, f32[8,64,2,128]{3,2,1,0:T(2,128)S(1)} %get-tuple-element.507, s32[]{:T(128)} %get-tuple-element.496), kind=kOutput, calls=%fused_computation.19.clone.1 | convolution fusion | flops 30408704 | bytes 197124 | tf_op jit(solution)/shard_map/while/body/eval_jaxpr/gbk,gck->gcb/dot_general | solution.py:50
  192.6 5.7 %fusion.214 = f32[8,64,2,128]{3,2,1,0:T(2,128)S(1)} fusion(f32[8,64,2,128]{3,2,1,0:T(2,128)S(1)} %get-tuple-element.498, s32[]{:T(128)} %get-tuple-element.496, f32[64,128]{1,0:T(8,128)S(1)} %fusion.212, f32[64,128]{1,0:T(8,128)S(1)} %multiply_add_fusion.38, f32[128]{0:T(128)S(1)} %iota_convert_fusion.4, f32[64,2,128]{2,0,1:T(8,128)S(1)} %maximum_multiply_fusion.6), kind=kOutput, calls=%fused_computation.31.clone.1 | convolution fusion | flops 30408704 | bytes 197124 | tf_op jit(solution)/shard_map/while/body/eval_jaxpr/gbk,gcb->gck/dot_general | solution.py:82
  200.7 2.6 gather_fusion
  203.2 3.0 broadcast_select_fusion
  207.3 16.7 %scatter_fusion = f32[2,2048,128]{2,0,1:T(2,128)S(1)} fusion(f32[2,2048,128]{2,0,1:T(2,128)S(1)} %broadcast.1542.clone, s32[512]{0:T(512)S(1)} %compare_select_fusion.2, f32[512,2,128]{2,1,0:T(2,128)S(1)} %bitcast.161), kind=kCustom, calls=%fused_computation.4 | custom fusion | flops 131072 | bytes 1574912 | tf_op jit(solution)/shard_map/scatter-add | solution.py:138
  225.7 5.9 %all-to-all-start = ((f32[512,5,128]{2,1,0:T(8,128)}), f32[512,5,128]{2,1,0:T(8,128)}, u32[]{:S(2)}, u32[]{:S(2)}) async-start(f32[512,5,128]{2,1,0:T(8,128)} %broadcast_select_fusion), calls=%async_computation | async-start | bytes 4194304 | tf_op jit(solution)/shard_map/all_to_all | solution.py:151
  233.6 13.0 %subtract_multiply_fusion.12 = (f32[4,64,32,128]{3,1,2,0:T(8,128)S(1)}, f32[4,64,32,128]{3,1,2,0:T(8,128)S(1)}, f32[4,64,32,128]{3,1,2,0:T(8,128)S(1)}) fusion(f32[4,64,1,128]{3,1,2,0:T(8,128)S(1)} %collective-permute-done.2, f32[4,64,32,128]{3,1,2,0:T(8,128)} %copy-done.2, f32[4,64,1,128]{3,1,2,0:T(8,128)S(1)} %collective-permute-done.3, ...), kind=kLoop, calls=%fused_computation.262 | loop fusion | flops 10485760 | bytes 17170432 | tf_op jit(solution)/shard_map/mul | solution.py:105
  246.7 4.1 fusion.165
  250.8 5.5 %fusion.161 = f32[4,64,32,128]{3,1,2,0:T(8,128)S(1)} fusion(f32[4,64,32,128]{3,1,2,0:T(8,128)S(1)} %copy-done.3, f32[1,64,32,128]{3,1,2,0:T(8,128)} %get-tuple-element.364, f32[1,64,32,128]{3,1,2,0:T(8,128)} %get-tuple-element.363, f32[1,64,32,128]{3,1,2,0:T(8,128)} %get-tuple-element.375, f32[1,64,32,128]{3,1,2,0:T(8,128)S(1)} %get-tuple-element.362, ...), kind=kLoop, calls=%fused_computation.254 | loop fusion | flops 18874368 | bytes 12976128 | tf_op jit(solution)/shard_map/add | solution.py:115
  260.0 2.9 collective-permute-start.4
  262.9 3.0 collective-permute-start.5
  268.2 2.5 broadcast_select_fusion.1
  270.7 8.6 %collective-permute-done.6 = f32[4,64,1,128]{3,1,2,0:T(8,128)S(1)} collective-permute-done((f32[4,64,1,128]{3,1,2,0:T(8,128)S(1)}, f32[4,64,1,128]{3,1,2,0:T(8,128)S(1)}, u32[]{:S(2)}, u32[]{:S(2)}) %collective-permute-start.6) | collective-permute-done | bytes 131104 | tf_op jit(solution)/shard_map/ppermute | solution.py:33
  279.3 3.0 collective-permute-done.7
  282.3 15.8 %subtract_multiply_fusion.9 = (f32[4,64,32,128]{3,1,2,0:T(8,128)}, f32[4,64,32,128]{3,1,2,0:T(8,128)}, f32[4,64,32,128]{3,1,2,0:T(8,128)}) fusion(f32[4,64,1,128]{3,1,2,0:T(8,128)S(1)} %collective-permute-done.6, f32[4,64,32,128]{3,1,2,0:T(8,128)} %copy-done, f32[4,64,1,128]{3,1,2,0:T(8,128)S(1)} %collective-permute-done.7, ...), kind=kLoop, calls=%fused_computation.259 | loop fusion | flops 10485760 | bytes 17170432 | tf_op jit(solution)/shard_map/mul | solution.py:105
  300.2 167.2 %while.31 = (s32[]{:T(128)}, f32[8,64,5,128]{3,1,0,2:T(8,128)S(1)}, f32[8,64,2,128]{3,2,1,0:T(2,128)S(1)}, f32[8,64,5,128]{3,1,2,0:T(8,128)S(1)}, f32[8,64,2,128]{3,2,1,0:T(2,128)}, /*index=5*/f32[8,64]{1,0:T(8,128)}, s32[]{:T(128)}) while((s32[]{:T(128)}, f32[8,64,5,128]{3,1,0,2:T(8,128)S(1)}, f32[8,64,2,128]{3,2,1,0:T(2,128)S(1)}, ...), condition=%wide.region_8.10_spmd, body=%wide.region_5.9_spmd.sunk | while | flops 73212032 | bytes 2330461 | solution.py:90
  302.7 9.1 %fusion.220 = f32[64,2,128]{2,1,0:T(2,128)S(1)} fusion(f32[64,128]{1,0:T(8,128)S(1)} %fusion.219, f32[128]{0:T(128)S(1)} %iota_convert_fusion.5, f32[64,128]{1,0:T(8,128)S(1)} %slice_bitcast_fusion.5, f32[8,64,2,128]{3,2,1,0:T(2,128)} %get-tuple-element.528, s32[]{:T(128)} %get-tuple-element.517), kind=kOutput, calls=%fused_computation.136.clone.1 | convolution fusion | flops 30408704 | bytes 197632 | tf_op jit(solution)/shard_map/while/body/eval_jaxpr/gbk,gck->gcb/dot_general | solution.py:50
  315.3 5.7 %fusion.226 = f32[8,64,2,128]{3,2,1,0:T(2,128)S(1)} fusion(f32[8,64,2,128]{3,2,1,0:T(2,128)S(1)} %get-tuple-element.519, s32[]{:T(128)} %get-tuple-element.517, f32[64,128]{1,0:T(8,128)S(1)} %fusion.224, f32[64,128]{1,0:T(8,128)S(1)} %multiply_add_fusion.39, f32[128]{0:T(128)S(1)} %iota_convert_fusion.5, f32[64,2,128]{2,0,1:T(8,128)S(1)} %maximum_multiply_fusion.7), kind=kOutput, calls=%fused_computation.148.clone.1 | convolution fusion | flops 30408704 | bytes 197124 | tf_op jit(solution)/shard_map/while/body/eval_jaxpr/gbk,gcb->gck/dot_general | solution.py:82
  321.2 2.4 fusion.219
  323.6 9.1 %fusion.220 = f32[64,2,128]{2,1,0:T(2,128)S(1)} fusion(f32[64,128]{1,0:T(8,128)S(1)} %fusion.219, f32[128]{0:T(128)S(1)} %iota_convert_fusion.5, f32[64,128]{1,0:T(8,128)S(1)} %slice_bitcast_fusion.5, f32[8,64,2,128]{3,2,1,0:T(2,128)} %get-tuple-element.528, s32[]{:T(128)} %get-tuple-element.517), kind=kOutput, calls=%fused_computation.136.clone.1 | convolution fusion | flops 30408704 | bytes 197632 | tf_op jit(solution)/shard_map/while/body/eval_jaxpr/gbk,gck->gcb/dot_general | solution.py:50
  333.8 2.4 fusion.224
  336.2 5.7 %fusion.226 = f32[8,64,2,128]{3,2,1,0:T(2,128)S(1)} fusion(f32[8,64,2,128]{3,2,1,0:T(2,128)S(1)} %get-tuple-element.519, s32[]{:T(128)} %get-tuple-element.517, f32[64,128]{1,0:T(8,128)S(1)} %fusion.224, f32[64,128]{1,0:T(8,128)S(1)} %multiply_add_fusion.39, f32[128]{0:T(128)S(1)} %iota_convert_fusion.5, f32[64,2,128]{2,0,1:T(8,128)S(1)} %maximum_multiply_fusion.7), kind=kOutput, calls=%fused_computation.148.clone.1 | convolution fusion | flops 30408704 | bytes 197124 | tf_op jit(solution)/shard_map/while/body/eval_jaxpr/gbk,gcb->gck/dot_general | solution.py:82
  342.1 2.4 fusion.219
  344.5 9.1 %fusion.220 = f32[64,2,128]{2,1,0:T(2,128)S(1)} fusion(f32[64,128]{1,0:T(8,128)S(1)} %fusion.219, f32[128]{0:T(128)S(1)} %iota_convert_fusion.5, f32[64,128]{1,0:T(8,128)S(1)} %slice_bitcast_fusion.5, f32[8,64,2,128]{3,2,1,0:T(2,128)} %get-tuple-element.528, s32[]{:T(128)} %get-tuple-element.517), kind=kOutput, calls=%fused_computation.136.clone.1 | convolution fusion | flops 30408704 | bytes 197632 | tf_op jit(solution)/shard_map/while/body/eval_jaxpr/gbk,gck->gcb/dot_general | solution.py:50
  354.7 2.4 fusion.224
  357.1 5.7 %fusion.226 = f32[8,64,2,128]{3,2,1,0:T(2,128)S(1)} fusion(f32[8,64,2,128]{3,2,1,0:T(2,128)S(1)} %get-tuple-element.519, s32[]{:T(128)} %get-tuple-element.517, f32[64,128]{1,0:T(8,128)S(1)} %fusion.224, f32[64,128]{1,0:T(8,128)S(1)} %multiply_add_fusion.39, f32[128]{0:T(128)S(1)} %iota_convert_fusion.5, f32[64,2,128]{2,0,1:T(8,128)S(1)} %maximum_multiply_fusion.7), kind=kOutput, calls=%fused_computation.148.clone.1 | convolution fusion | flops 30408704 | bytes 197124 | tf_op jit(solution)/shard_map/while/body/eval_jaxpr/gbk,gcb->gck/dot_general | solution.py:82
  365.4 9.1 %fusion.220 = f32[64,2,128]{2,1,0:T(2,128)S(1)} fusion(f32[64,128]{1,0:T(8,128)S(1)} %fusion.219, f32[128]{0:T(128)S(1)} %iota_convert_fusion.5, f32[64,128]{1,0:T(8,128)S(1)} %slice_bitcast_fusion.5, f32[8,64,2,128]{3,2,1,0:T(2,128)} %get-tuple-element.528, s32[]{:T(128)} %get-tuple-element.517), kind=kOutput, calls=%fused_computation.136.clone.1 | convolution fusion | flops 30408704 | bytes 197632 | tf_op jit(solution)/shard_map/while/body/eval_jaxpr/gbk,gck->gcb/dot_general | solution.py:50
  378.0 5.7 %fusion.226 = f32[8,64,2,128]{3,2,1,0:T(2,128)S(1)} fusion(f32[8,64,2,128]{3,2,1,0:T(2,128)S(1)} %get-tuple-element.519, s32[]{:T(128)} %get-tuple-element.517, f32[64,128]{1,0:T(8,128)S(1)} %fusion.224, f32[64,128]{1,0:T(8,128)S(1)} %multiply_add_fusion.39, f32[128]{0:T(128)S(1)} %iota_convert_fusion.5, f32[64,2,128]{2,0,1:T(8,128)S(1)} %maximum_multiply_fusion.7), kind=kOutput, calls=%fused_computation.148.clone.1 | convolution fusion | flops 30408704 | bytes 197124 | tf_op jit(solution)/shard_map/while/body/eval_jaxpr/gbk,gcb->gck/dot_general | solution.py:82
  383.9 2.4 fusion.219
  386.3 9.1 %fusion.220 = f32[64,2,128]{2,1,0:T(2,128)S(1)} fusion(f32[64,128]{1,0:T(8,128)S(1)} %fusion.219, f32[128]{0:T(128)S(1)} %iota_convert_fusion.5, f32[64,128]{1,0:T(8,128)S(1)} %slice_bitcast_fusion.5, f32[8,64,2,128]{3,2,1,0:T(2,128)} %get-tuple-element.528, s32[]{:T(128)} %get-tuple-element.517), kind=kOutput, calls=%fused_computation.136.clone.1 | convolution fusion | flops 30408704 | bytes 197632 | tf_op jit(solution)/shard_map/while/body/eval_jaxpr/gbk,gck->gcb/dot_general | solution.py:50
  396.5 2.4 fusion.224
  398.9 5.7 %fusion.226 = f32[8,64,2,128]{3,2,1,0:T(2,128)S(1)} fusion(f32[8,64,2,128]{3,2,1,0:T(2,128)S(1)} %get-tuple-element.519, s32[]{:T(128)} %get-tuple-element.517, f32[64,128]{1,0:T(8,128)S(1)} %fusion.224, f32[64,128]{1,0:T(8,128)S(1)} %multiply_add_fusion.39, f32[128]{0:T(128)S(1)} %iota_convert_fusion.5, f32[64,2,128]{2,0,1:T(8,128)S(1)} %maximum_multiply_fusion.7), kind=kOutput, calls=%fused_computation.148.clone.1 | convolution fusion | flops 30408704 | bytes 197124 | tf_op jit(solution)/shard_map/while/body/eval_jaxpr/gbk,gcb->gck/dot_general | solution.py:82
  404.8 2.4 fusion.219
  407.2 9.1 %fusion.220 = f32[64,2,128]{2,1,0:T(2,128)S(1)} fusion(f32[64,128]{1,0:T(8,128)S(1)} %fusion.219, f32[128]{0:T(128)S(1)} %iota_convert_fusion.5, f32[64,128]{1,0:T(8,128)S(1)} %slice_bitcast_fusion.5, f32[8,64,2,128]{3,2,1,0:T(2,128)} %get-tuple-element.528, s32[]{:T(128)} %get-tuple-element.517), kind=kOutput, calls=%fused_computation.136.clone.1 | convolution fusion | flops 30408704 | bytes 197632 | tf_op jit(solution)/shard_map/while/body/eval_jaxpr/gbk,gck->gcb/dot_general | solution.py:50
  419.8 5.7 %fusion.226 = f32[8,64,2,128]{3,2,1,0:T(2,128)S(1)} fusion(f32[8,64,2,128]{3,2,1,0:T(2,128)S(1)} %get-tuple-element.519, s32[]{:T(128)} %get-tuple-element.517, f32[64,128]{1,0:T(8,128)S(1)} %fusion.224, f32[64,128]{1,0:T(8,128)S(1)} %multiply_add_fusion.39, f32[128]{0:T(128)S(1)} %iota_convert_fusion.5, f32[64,2,128]{2,0,1:T(8,128)S(1)} %maximum_multiply_fusion.7), kind=kOutput, calls=%fused_computation.148.clone.1 | convolution fusion | flops 30408704 | bytes 197124 | tf_op jit(solution)/shard_map/while/body/eval_jaxpr/gbk,gcb->gck/dot_general | solution.py:82
  428.1 9.1 %fusion.220 = f32[64,2,128]{2,1,0:T(2,128)S(1)} fusion(f32[64,128]{1,0:T(8,128)S(1)} %fusion.219, f32[128]{0:T(128)S(1)} %iota_convert_fusion.5, f32[64,128]{1,0:T(8,128)S(1)} %slice_bitcast_fusion.5, f32[8,64,2,128]{3,2,1,0:T(2,128)} %get-tuple-element.528, s32[]{:T(128)} %get-tuple-element.517), kind=kOutput, calls=%fused_computation.136.clone.1 | convolution fusion | flops 30408704 | bytes 197632 | tf_op jit(solution)/shard_map/while/body/eval_jaxpr/gbk,gck->gcb/dot_general | solution.py:50
  440.7 5.7 %fusion.226 = f32[8,64,2,128]{3,2,1,0:T(2,128)S(1)} fusion(f32[8,64,2,128]{3,2,1,0:T(2,128)S(1)} %get-tuple-element.519, s32[]{:T(128)} %get-tuple-element.517, f32[64,128]{1,0:T(8,128)S(1)} %fusion.224, f32[64,128]{1,0:T(8,128)S(1)} %multiply_add_fusion.39, f32[128]{0:T(128)S(1)} %iota_convert_fusion.5, f32[64,2,128]{2,0,1:T(8,128)S(1)} %maximum_multiply_fusion.7), kind=kOutput, calls=%fused_computation.148.clone.1 | convolution fusion | flops 30408704 | bytes 197124 | tf_op jit(solution)/shard_map/while/body/eval_jaxpr/gbk,gcb->gck/dot_general | solution.py:82
  449.0 9.1 %fusion.220 = f32[64,2,128]{2,1,0:T(2,128)S(1)} fusion(f32[64,128]{1,0:T(8,128)S(1)} %fusion.219, f32[128]{0:T(128)S(1)} %iota_convert_fusion.5, f32[64,128]{1,0:T(8,128)S(1)} %slice_bitcast_fusion.5, f32[8,64,2,128]{3,2,1,0:T(2,128)} %get-tuple-element.528, s32[]{:T(128)} %get-tuple-element.517), kind=kOutput, calls=%fused_computation.136.clone.1 | convolution fusion | flops 30408704 | bytes 197632 | tf_op jit(solution)/shard_map/while/body/eval_jaxpr/gbk,gck->gcb/dot_general | solution.py:50
  461.6 5.7 %fusion.226 = f32[8,64,2,128]{3,2,1,0:T(2,128)S(1)} fusion(f32[8,64,2,128]{3,2,1,0:T(2,128)S(1)} %get-tuple-element.519, s32[]{:T(128)} %get-tuple-element.517, f32[64,128]{1,0:T(8,128)S(1)} %fusion.224, f32[64,128]{1,0:T(8,128)S(1)} %multiply_add_fusion.39, f32[128]{0:T(128)S(1)} %iota_convert_fusion.5, f32[64,2,128]{2,0,1:T(8,128)S(1)} %maximum_multiply_fusion.7), kind=kOutput, calls=%fused_computation.148.clone.1 | convolution fusion | flops 30408704 | bytes 197124 | tf_op jit(solution)/shard_map/while/body/eval_jaxpr/gbk,gcb->gck/dot_general | solution.py:82
  468.8 32.1 %scatter_fusion.1 = f32[2,2048,128]{2,0,1:T(2,128)S(1)} fusion(f32[2,2048,128]{2,0,1:T(2,128)S(1)} %broadcast.1542, s32[512]{0:T(512)S(1)} %compare_select_fusion.1, f32[512,2,128]{2,1,0:T(2,128)} %bitcast.162), kind=kCustom, calls=%fused_computation.5 | custom fusion | flops 131072 | bytes 1574912 | tf_op jit(solution)/shard_map/scatter-add | solution.py:138
  501.0 2.7 fusion.178
  503.7 3.7 fusion.164
  507.4 4.1 fusion.163
  511.6 4.4 copy.127
  (340 shorter events, 110.6 us)
Async XLA Ops:
  0.6 13.9 %copy-start.18 = (s32[512]{0:T(512)S(1)}, s32[512]{0:T(512)}, u32[]{:S(2)}) copy-start(s32[512]{0:T(512)} %param.15) | copy-start | bytes 6148
  5.3 9.3 %copy-start.2 = (f32[4,64,32,128]{3,1,2,0:T(8,128)}, f32[4,64,32,128]{3,1,2,0:T(8,128)S(1)}, u32[]{:S(2)}) copy-start(f32[4,64,32,128]{3,1,2,0:T(8,128)S(1)} %copy.117) | copy-start | bytes 12582916
  5.3 23.5 %copy-start.16 = (s32[512]{0:T(512)S(1)}, s32[512]{0:T(512)}, u32[]{:S(2)}) copy-start(s32[512]{0:T(512)} %param.16) | copy-start | bytes 6148
  5.3 228.2 %collective-permute-start.2 = (f32[4,64,1,128]{3,1,2,0:T(8,128)S(1)}, f32[4,64,1,128]{3,1,2,0:T(8,128)S(1)}, u32[]{:S(2)}, u32[]{:S(2)}) collective-permute-start(f32[4,64,1,128]{3,1,2,0:T(8,128)S(1)} %get-tuple-element.382), channel_id=1, source_target_pairs={{1,0},{2,1},{3,2},{4,3},{5,4},{6,5},{7,6},{0,7},{9,8},{10,9},{11,1... | collective-permute-start | bytes 393224 | tf_op jit(solution)/shard_map/ppermute | solution.py:33
  6.5 227.1 %collective-permute-start.3 = (f32[4,64,1,128]{3,1,2,0:T(8,128)S(1)}, f32[4,64,1,128]{3,1,2,0:T(8,128)S(1)}, u32[]{:S(2)}, u32[]{:S(2)}) collective-permute-start(f32[4,64,1,128]{3,1,2,0:T(8,128)S(1)} %get-tuple-element.381), channel_id=1, source_target_pairs={{0,1},{1,2},{2,3},{3,4},{4,5},{5,6},{6,7},{7,0},{8,9},{9,10},{10,1... | collective-permute-start | bytes 393224 | tf_op jit(solution)/shard_map/ppermute | solution.py:31
  7.7 225.8 %collective-permute-start = (f32[4,1,32,128]{3,1,2,0:T(1,128)S(1)}, f32[4,1,32,128]{3,1,2,0:T(1,128)S(1)}, u32[]{:S(2)}, u32[]{:S(2)}) collective-permute-start(f32[4,1,32,128]{3,1,2,0:T(1,128)S(1)} %bitcast.171), channel_id=1, source_target_pairs={{8,0},{16,8},{24,16},{9,1},{17,9},{25,17},{10,2},{18,10},{26,18},{... | collective-permute-start | bytes 196616 | tf_op jit(solution)/shard_map/ppermute | solution.py:33
  10.9 222.7 %collective-permute-start.1 = (f32[4,1,32,128]{3,1,2,0:T(1,128)S(1)}, f32[4,1,32,128]{3,1,2,0:T(1,128)S(1)}, u32[]{:S(2)}, u32[]{:S(2)}) collective-permute-start(f32[4,1,32,128]{3,1,2,0:T(1,128)S(1)} %bitcast.170), channel_id=1, source_target_pairs={{0,8},{8,16},{16,24},{1,9},{9,17},{17,25},{2,10},{10,18},{18,26},{... | collective-permute-start | bytes 196616 | tf_op jit(solution)/shard_map/ppermute | solution.py:31
  18.8 206.8 %all-to-all-start.1 = ((f32[32,16,1]{1,2,0:T(1,128)}), f32[32,16,1]{1,2,0:T(1,128)S(1)}, u32[]{:S(2)}, u32[]{:S(2)}) async-start(f32[32,16,1]{1,2,0:T(1,128)} %bitcast.48), calls=%async_computation.1 | async-start | bytes 32768 | tf_op jit(solution)/shard_map/all_to_all | solution.py:152
  35.1 163.4 %copy-start.17 = (s32[512]{0:T(512)S(1)}, s32[512]{0:T(512)}, u32[]{:S(2)}) copy-start(s32[512]{0:T(512)} %param.17) | copy-start | bytes 6148
  225.7 72.4 %all-to-all-start = ((f32[512,5,128]{2,1,0:T(8,128)}), f32[512,5,128]{2,1,0:T(8,128)}, u32[]{:S(2)}, u32[]{:S(2)}) async-start(f32[512,5,128]{2,1,0:T(8,128)} %broadcast_select_fusion), calls=%async_computation | async-start | bytes 4194304 | tf_op jit(solution)/shard_map/all_to_all | solution.py:151
  233.5 13.1 %copy-start.10 = (f32[4,1,32,128]{3,1,2,0:T(1,128)}, f32[4,1,32,128]{3,1,2,0:T(1,128)S(1)}, u32[]{:S(2)}) copy-start(f32[4,1,32,128]{3,1,2,0:T(1,128)S(1)} %collective-permute-done) | copy-start | bytes 196612
  233.5 13.1 %copy-start.11 = (f32[4,1,32,128]{3,1,2,0:T(1,128)}, f32[4,1,32,128]{3,1,2,0:T(1,128)S(1)}, u32[]{:S(2)}) copy-start(f32[4,1,32,128]{3,1,2,0:T(1,128)S(1)} %collective-permute-done.1) | copy-start | bytes 196612
  233.6 13.1 %copy-start.6 = (f32[4,64,1,128]{3,1,2,0:T(8,128)}, f32[4,64,1,128]{3,1,2,0:T(8,128)S(1)}, u32[]{:S(2)}) copy-start(f32[4,64,1,128]{3,1,2,0:T(8,128)S(1)} %collective-permute-done.2) | copy-start | bytes 393220
  233.6 13.1 %copy-start.7 = (f32[4,64,1,128]{3,1,2,0:T(8,128)}, f32[4,64,1,128]{3,1,2,0:T(8,128)S(1)}, u32[]{:S(2)}) copy-start(f32[4,64,1,128]{3,1,2,0:T(8,128)S(1)} %collective-permute-done.3) | copy-start | bytes 393220
  246.7 4.1 copy-start.3
  256.3 3.6 copy-start
  256.5 11.7 %copy-start.19 = (pred[512]{0:T(512)(128)(4,1)S(1)}, pred[512]{0:T(512)(128)(4,1)}, u32[]{:S(2)}) copy-start(pred[512]{0:T(512)(128)(4,1)} %compare_and_fusion) | copy-start | bytes 1540
  258.4 20.9 %collective-permute-start.6 = (f32[4,64,1,128]{3,1,2,0:T(8,128)S(1)}, f32[4,64,1,128]{3,1,2,0:T(8,128)S(1)}, u32[]{:S(2)}, u32[]{:S(2)}) collective-permute-start(f32[4,64,1,128]{3,1,2,0:T(8,128)S(1)} %get-tuple-element.372), channel_id=1, source_target_pairs={{1,0},{2,1},{3,2},{4,3},{5,4},{6,5},{7,6},{0,7},{9,8},{10,9},{11,1... | collective-permute-start | bytes 393224 | tf_op jit(solution)/shard_map/ppermute | solution.py:33
  259.6 22.7 %collective-permute-start.7 = (f32[4,64,1,128]{3,1,2,0:T(8,128)S(1)}, f32[4,64,1,128]{3,1,2,0:T(8,128)S(1)}, u32[]{:S(2)}, u32[]{:S(2)}) collective-permute-start(f32[4,64,1,128]{3,1,2,0:T(8,128)S(1)} %get-tuple-element.371), channel_id=1, source_target_pairs={{0,1},{1,2},{2,3},{3,4},{4,5},{5,6},{6,7},{7,0},{8,9},{9,10},{10,1... | collective-permute-start | bytes 393224 | tf_op jit(solution)/shard_map/ppermute | solution.py:31
  260.0 10.7 %collective-permute-start.4 = (f32[4,1,32,128]{3,1,2,0:T(1,128)S(1)}, f32[4,1,32,128]{3,1,2,0:T(1,128)S(1)}, u32[]{:S(2)}, u32[]{:S(2)}) collective-permute-start(f32[4,1,32,128]{3,1,2,0:T(1,128)S(1)} %get-tuple-element.374), channel_id=1, source_target_pairs={{8,0},{16,8},{24,16},{9,1},{17,9},{25,17},{10,2},{18,10},{26,18},{... | collective-permute-start | bytes 196616 | tf_op jit(solution)/shard_map/ppermute | solution.py:33
  262.9 7.8 %collective-permute-start.5 = (f32[4,1,32,128]{3,1,2,0:T(1,128)S(1)}, f32[4,1,32,128]{3,1,2,0:T(1,128)S(1)}, u32[]{:S(2)}, u32[]{:S(2)}) collective-permute-start(f32[4,1,32,128]{3,1,2,0:T(1,128)S(1)} %get-tuple-element.373), channel_id=1, source_target_pairs={{0,8},{8,16},{16,24},{1,9},{9,17},{17,25},{2,10},{10,18},{18,26},{... | collective-permute-start | bytes 196616 | tf_op jit(solution)/shard_map/ppermute | solution.py:31
  270.7 27.4 %copy-start.12 = (f32[4,1,32,128]{3,1,2,0:T(1,128)}, f32[4,1,32,128]{3,1,2,0:T(1,128)S(1)}, u32[]{:S(2)}) copy-start(f32[4,1,32,128]{3,1,2,0:T(1,128)S(1)} %collective-permute-done.4) | copy-start | bytes 196612
  270.7 27.4 %copy-start.14 = (f32[4,1,32,128]{3,1,2,0:T(1,128)}, f32[4,1,32,128]{3,1,2,0:T(1,128)S(1)}, u32[]{:S(2)}) copy-start(f32[4,1,32,128]{3,1,2,0:T(1,128)S(1)} %collective-permute-done.5) | copy-start | bytes 196612
  282.3 15.8 %copy-start.8 = (f32[4,64,1,128]{3,1,2,0:T(8,128)}, f32[4,64,1,128]{3,1,2,0:T(8,128)S(1)}, u32[]{:S(2)}) copy-start(f32[4,64,1,128]{3,1,2,0:T(8,128)S(1)} %collective-permute-done.7) | copy-start | bytes 393220
  467.5 0.8 copy-start.5
  501.0 2.7 copy-start.4
  503.7 3.7 copy-start.1
  503.7 3.7 copy-start.9
  503.7 3.7 copy-start.13
  503.7 3.7 copy-start.15
where the time goes:
time: 525 us; the launch traced here: 517 us
  matrix products  230 us (44%)
  other arithmetic  189 us (36%)
  local copies, waits for them, and re-layouts  53.6 us (10%)
  starting transfers between devices  29.2 us (6%)
  waiting for transfers between devices  11.6 us (2%)
    dot_general x16, matrix products, advance_group(): jnp.einsum('gbk,gck->gcb', weights, tile_row_count, precision=lax.Precisi...  139 us
    dot_general x16, matrix products, advance_group(): jnp.einsum('gbk,gcb->gck', weights, source_amounts, precision=lax.Precisi...  90.8 us
    reduce_sum x32, other arithmetic, kernel_weights(): return raw / jnp.sum(raw, axis=-1, keepdims=True)  75.5 us
    scatter-add x2, other arithmetic, local_update(): jnp.zeros_like(selected).at[:, tile_indices]  48.8 us
    mul x2, other arithmetic, fluid_update(): d_azim = 0.5 * (azim_up - azim_down)  28.8 us
  transfers between devices with their start and end apart: 10, of which 2 were waited for; matrix products, arithmetic and copies ran while one was open for 48% of the time, Pallas kernels for 0%

commit v1 on v0

v1 whole, which is shorter than its diff:
```python
import functools

import jax
import jax.numpy as jnp
from jax import lax
from jax.experimental import pallas as pl
from jax.experimental.pallas import tpu as pltpu
from jax.sharding import PartitionSpec as P

SUBSTEPS = 8
TIME_STEP = 0.25
MEAN_FLOW = 0.5
DIFFUSION = 0.1
KERNEL_WIDTH = 1.5
GAS_INDEX = 4.2
PRESSURE_COUPLING = 0.3
AMBIENT = 1.0
RELAX_TIME = 0.5
VISCOUS = 0.08
SOURCE_GAIN = 0.05
VOID_SCALE = 0.01
FOUR_PI = 12.566370614359172
GROUP = 8
STATES = 5
ROWS = GROUP * STATES
WIDE = 4


def split_bf16(values):
    high = values.astype(jnp.bfloat16)
    low = (values - high.astype(jnp.float32)).astype(jnp.bfloat16)
    return high, low


def stacked_lhs(rows):
    high = rows.astype(jnp.bfloat16).astype(jnp.float32)
    both = jnp.concatenate([high, rows - high], axis=0).astype(jnp.bfloat16)
    return jnp.concatenate([both, both], axis=1)


def raw_weights(position_row, cells):
    offset = cells - position_row
    return jnp.exp(offset * offset * (-0.5 / (KERNEL_WIDTH * KERNEL_WIDTH)))


def bubble_kernel(first, *refs):
    if first:
        (order_ref, tiles_ref, count_ref, bubbles_ref, p_ref, u_ref,
         state_ref, source_ref, sp, su, sn, amounts, rows) = refs
        void_ref = None
        old_ref = state_ref
    else:
        (tiles_ref, old_ref, p_ref, u_ref,
         bubbles_out, source_ref, void_ref, sp, su, sn, amounts, rows, state_ref) = refs
    cells_n, lanes = p_ref.shape[1:][-1], sp.shape[1]
    groups = sp.shape[0] // GROUP
    cells = lax.broadcasted_iota(jnp.int32, (cells_n, lanes), 0).astype(jnp.float32)
    source_ref[...] = jnp.zeros_like(source_ref)
    if void_ref is not None:
        void_ref[...] = jnp.zeros_like(void_ref)
    rows[...] = jnp.zeros_like(rows)
    amounts[...] = jnp.zeros_like(amounts)
    for pair in range(GROUP // 2):
        rows[8 * pair + 2 : 8 * pair + 3, :] = jnp.ones((1, cells_n), jnp.float32)

    if first:
        state_row = lax.broadcasted_iota(jnp.int32, (STATES, lanes), 0)
        marker = jnp.where(state_row == 0, -1.0, 1.0)

    def tile_of(slot):
        return tiles_ref[order_ref[slot]] if first else tiles_ref[slot]

    def sample(g, carry):
        base = g * GROUP
        for j in range(GROUP):
            tile = tile_of(base + j)
            if first:
                block = order_ref[base + j]
                block_state = jnp.where(block < count_ref[0], bubbles_ref[block], marker)
                state_ref[pl.ds(g * ROWS + j, STATES, stride=GROUP), :] = block_state
            at = 4 * j
            rows[at : at + 1, :] = p_ref[0, pl.ds(tile, 1), :]
            rows[at + 1 : at + 2, :] = u_ref[0, pl.ds(tile, 1), :]
        for pair in range(GROUP // 2):
            highs, lows = [], []
            for j in (2 * pair, 2 * pair + 1):
                position = old_ref[pl.ds(g * ROWS + 2 * GROUP + j, 1), :]
                high, low = split_bf16(raw_weights(position, cells))
                highs.append(high)
                lows.append(low)
            rhs = jnp.concatenate(
                [jnp.concatenate(highs, axis=1), jnp.concatenate(lows, axis=1)], axis=0
            )
            lhs = stacked_lhs(rows[8 * pair : 8 * pair + 8, :])
            result = jnp.dot(lhs, rhs, preferred_element_type=jnp.float32)
            result = result[:8] + result[8:]
            for side in range(2):
                part = result[:, side * lanes : (side + 1) * lanes]
                at = base + 2 * pair + side
                sp[pl.ds(at, 1), :] = part[4 * side : 4 * side + 1]
                su[pl.ds(at, 1), :] = part[4 * side + 1 : 4 * side + 2]
                sn[pl.ds(at, 1), :] = part[2:3]
        return carry

    lax.fori_loop(0, groups, sample, 0)

    def advance(w, carry):
        for i in range(WIDE):
            g = w * WIDE + i
            row = pl.multiple_of(g * GROUP, GROUP)
            at = [pl.multiple_of(g * ROWS + c * GROUP, GROUP) for c in range(STATES)]
            radius, growth, position, speed, rest = (
                old_ref[pl.ds(a, GROUP), :] for a in at
            )
            live = radius * rest >= 0.0
            radius = jnp.where(live, radius, 1.0)
            inverse = 1.0 / sn[pl.ds(row, GROUP), :]
            pressure = sp[pl.ds(row, GROUP), :] * inverse
            velocity = su[pl.ds(row, GROUP), :] * inverse
            drive = AMBIENT + PRESSURE_COUPLING * pressure
            h = TIME_STEP / SUBSTEPS
            for _ in range(SUBSTEPS):
                over = 1.0 / radius
                gas = jnp.exp(GAS_INDEX * jnp.log(rest * over))
                accel = (gas - drive - 1.5 * growth * growth - VISCOUS * growth * over) * over
                growth = growth + h * accel
                radius = radius + h * growth
                speed = speed + (h / RELAX_TIME) * (velocity - speed)
                position = position + h * speed
            source = SOURCE_GAIN * FOUR_PI * radius * radius * growth
            amounts[pl.ds(g * 4 * GROUP, GROUP, stride=4), :] = jnp.where(live, source, 0.0)
            if first:
                radius = jnp.where(live, radius, -1.0)
                new = (radius, growth, position, speed, rest)
            else:
                void = VOID_SCALE * FOUR_PI / 3.0 * radius * radius * radius
                amounts[pl.ds(g * 4 * GROUP + 1, GROUP, stride=4), :] = jnp.where(live, void, 0.0)
                new = tuple(
                    jnp.where(live, x, 0.0) for x in (radius, growth, position, speed, rest)
                )
            for a, x in zip(at, new):
                state_ref[pl.ds(a, GROUP), :] = x
        return carry

    lax.fori_loop(0, groups // WIDE, advance, 0)

    def spread(g, carry):
        base = g * GROUP
        sublane = lax.broadcasted_iota(jnp.int32, (8, lanes), 0)
        for pair in range(GROUP // 2):
            pieces, norms = [], []
            for j in (2 * pair, 2 * pair + 1):
                position = state_ref[pl.ds(g * ROWS + 2 * GROUP + j, 1), :]
                raw = raw_weights(position, cells)
                norms.append(jnp.sum(raw, axis=0, keepdims=True))
                pieces.append(jnp.concatenate(split_bf16(raw), axis=1))
            rhs = jnp.concatenate(pieces, axis=0)
            amount = amounts[pl.ds(pl.multiple_of(g * 4 * GROUP + 8 * pair, 8), 8), :]
            amount = amount / jnp.where(sublane < 4, norms[0], norms[1])
            result = lax.dot_general(
                stacked_lhs(amount), rhs, (((1,), (1,)), ((), ())),
                preferred_element_type=jnp.float32,
            )
            result = result[:8] + result[8:]
            for side in range(2):
                part = result[:, side * cells_n : (side + 1) * cells_n]
                slot = base + 2 * pair + side
                tile = tile_of(slot)
                source_ref[pl.ds(tile, 1), :] += part[4 * side : 4 * side + 1]
                if void_ref is not None:
                    void_ref[pl.ds(tile, 1), :] += part[4 * side + 1 : 4 * side + 2]
                    bubbles_out[slot] = state_ref[
                        pl.ds(g * ROWS + 2 * pair + side, STATES, stride=GROUP), :
                    ]
        return carry

    lax.fori_loop(0, groups, spread, 0)


def bubble_step(first, fluid, scalars, state):
    comps, tiles, cells = fluid.shape
    lanes = state.shape[-1]
    slots = scalars[0].shape[0]
    field = jax.ShapeDtypeStruct((tiles, cells), jnp.float32)
    packed = (slots * STATES, lanes)
    scratch = [pltpu.VMEM((slots, lanes), jnp.float32) for _ in range(3)]
    scratch += [pltpu.VMEM((4 * slots, lanes), jnp.float32), pltpu.VMEM((32, cells), jnp.float32)]
    if first:
        outs = (jax.ShapeDtypeStruct(packed, jnp.float32), field)
    else:
        outs = (jax.ShapeDtypeStruct((slots, STATES, lanes), jnp.float32), field, field)
        scratch.append(pltpu.VMEM(packed, jnp.float32))
    whole = lambda shape: pl.BlockSpec(shape, lambda i: (0,) * len(shape))
    work = slots * lanes * cells
    return pl.pallas_call(
        functools.partial(bubble_kernel, first),
        grid=(1,),
        out_shape=outs,
        in_specs=[pl.BlockSpec(memory_space=pltpu.SMEM)] * len(scalars)
        + [
            whole(state.shape),
            pl.BlockSpec((1, tiles, cells), lambda i: (0, 0, 0)),
            pl.BlockSpec((1, tiles, cells), lambda i: (3, 0, 0)),
        ],
        out_specs=tuple(whole(o.shape) for o in outs),
        scratch_shapes=scratch,
        compiler_params=pltpu.CompilerParams(vmem_limit_bytes=40 * 2**20),
        cost_estimate=pl.CostEstimate(
            flops=work * 40, bytes_accessed=12 * 2**20, transcendentals=2 * work
        ),
        name="bubbles_first" if first else "bubbles_second",
    )(*scalars, state, fluid, fluid)


def fluid_kernel(edges, f_ref, before_ref, after_ref, low_ref, high_ref, left_ref, right_ref,
                 source_ref, out_ref, *edge_refs):
    step, steps = pl.program_id(0), pl.num_programs(0)
    comps, depth, width, cells = f_ref.shape
    row = lax.broadcasted_iota(jnp.int32, (width, cells), 0)
    lane = lax.broadcasted_iota(jnp.int32, (width, cells), 1)
    at_start, at_end = step == 0, step == steps - 1
    for s in range(depth):
        now, below, above = [], [], []
        for c in range(comps):
            now.append(f_ref[c, s])
            below.append(
                jnp.where(at_start, low_ref[c, 0], before_ref[c, 0]) if s == 0 else f_ref[c, s - 1]
            )
            above.append(
                jnp.where(at_end, high_ref[c, 0], after_ref[c, 0])
                if s == depth - 1
                else f_ref[c, s + 1]
            )
        d_s, d_a, d_r, lap = [], [], [], []
        for c in range(comps):
            x = now[c]
            a_down = jnp.where(row == 0, left_ref[c, s : s + 1, :], pltpu.roll(x, 1, 0))
            a_up = jnp.where(
                row == width - 1, right_ref[c, s : s + 1, :], pltpu.roll(x, width - 1, 0)
            )
            r_down = jnp.where(lane == 0, 0.0, pltpu.roll(x, 1, 1))
            r_up = jnp.where(lane == cells - 1, 0.0, pltpu.roll(x, cells - 1, 1))
            d_s.append(above[c] - below[c])
            d_a.append(a_up - a_down)
            d_r.append(r_up - r_down)
            lap.append(above[c] + below[c] + a_up + a_down + r_up + r_down - 6.0 * x)
        half = 0.5 * TIME_STEP
        change = [
            MEAN_FLOW * d_s[0] + d_s[1] + d_a[2] + d_r[3],
            MEAN_FLOW * d_s[1] + d_s[0],
            MEAN_FLOW * d_s[2] + d_a[0],
            MEAN_FLOW * d_s[3] + d_r[0],
        ]
        for c in range(comps):
            new = now[c] - half * change[c] + DIFFUSION * lap[c]
            if c == 0:
                new = new - TIME_STEP * source_ref[s]
            out_ref[c, s] = new
            if edges:
                edge_refs[0][c, s : s + 1, :] = new[0:1]
                edge_refs[1][c, s : s + 1, :] = new[width - 1 : width]


def fluid_step(edges, fluid, halos, source):
    comps, length, width, cells = fluid.shape
    depth = 8
    steps = length // depth
    plane = (comps, 1, width, cells)
    side = pl.BlockSpec((comps, depth, cells), lambda i: (0, i, 0))
    still = pl.BlockSpec(plane, lambda i: (0, 0, 0, 0))
    main = pl.BlockSpec((comps, depth, width, cells), lambda i: (0, i, 0, 0))
    outs = [jax.ShapeDtypeStruct(fluid.shape, jnp.float32)]
    out_specs = [main]
    if edges:
        outs += [jax.ShapeDtypeStruct((comps, length, cells), jnp.float32)] * 2
        out_specs += [side, side]
    return pl.pallas_call(
        functools.partial(fluid_kernel, edges),
        grid=(steps,),
        out_shape=tuple(outs),
        in_specs=[
            main,
            pl.BlockSpec(plane, lambda i: (0, jnp.maximum(i * depth - 1, 0), 0, 0)),
            pl.BlockSpec(plane, lambda i: (0, jnp.minimum(i * depth + depth, length - 1), 0, 0)),
            still,
            still,
            side,
            side,
            pl.BlockSpec((depth, width, cells), lambda i: (i, 0, 0)),
        ],
        out_specs=tuple(out_specs),
        compiler_params=pltpu.CompilerParams(vmem_limit_bytes=24 * 2**20),
        cost_estimate=pl.CostEstimate(
            flops=fluid.size * 30, bytes_accessed=10 * 2**20, transcendentals=0
        ),
        name="fluid_first" if edges else "fluid_second",
    )(fluid, fluid, fluid, *halos, source)


def exchange(fluid, first_col, last_col):
    streams, azims = lax.axis_size("stream"), lax.axis_size("azim")
    length = fluid.shape[1]
    up = [(i, i + 1) for i in range(streams - 1)]
    down = [(i + 1, i) for i in range(streams - 1)]
    right = [(i, (i + 1) % azims) for i in range(azims)]
    left = [((i + 1) % azims, i) for i in range(azims)]
    return (
        lax.ppermute(fluid[:, length - 1 :], "stream", up),
        lax.ppermute(fluid[:, :1], "stream", down),
        lax.ppermute(last_col, "azim", right),
        lax.ppermute(first_col, "azim", left),
    )


def on_device(fluid, bubbles, counts, outgoing_block_order, tiles_first_update, tiles_after):
    comps, length, width, cells = fluid.shape
    slots, states, lanes = bubbles.shape
    devices = lax.axis_size("stream") * lax.axis_size("azim")
    cap = slots // devices
    flat = (comps, length * width, cells)
    grid = (length, width, cells)
    halos = exchange(fluid, fluid[:, :, 0], fluid[:, :, width - 1])
    sent, source = bubble_step(
        True, fluid.reshape(flat), (outgoing_block_order, tiles_first_update, counts), bubbles
    )
    axes = ("stream", "azim")
    if cap % GROUP == 0:
        sent = sent.reshape(devices, cap * states, lanes)
        arrived = lax.all_to_all(sent, axes, split_axis=0, concat_axis=0, tiled=True)
    else:
        sent = sent.reshape(slots // GROUP, states, GROUP, lanes).transpose(0, 2, 1, 3)
        sent = sent.reshape(devices, cap * states, lanes)
        arrived = lax.all_to_all(sent, axes, split_axis=0, concat_axis=0, tiled=True)
        arrived = arrived.reshape(slots // GROUP, GROUP, states, lanes).transpose(0, 2, 1, 3)
    arrived = arrived.reshape(slots * states, lanes)
    fluid, first_col, last_col = fluid_step(True, fluid, halos, source.reshape(grid))
    halos = exchange(fluid, first_col, last_col)
    bubbles, source, void = bubble_step(False, fluid.reshape(flat), (tiles_after,), arrived)
    (fluid,) = fluid_step(False, fluid, halos, source.reshape(grid))
    return fluid, bubbles, void.reshape(grid)


def solution(mesh):
    return jax.shard_map(
        on_device,
        mesh=mesh,
        in_specs=(
            P(None, "stream", "azim", None),
            P(("stream", "azim"), None, None),
            P(("stream", "azim")),
            P(("stream", "azim")),
            P(("stream", "azim")),
            P(("stream", "azim")),
        ),
        out_specs=(
            P(None, "stream", "azim", None),
            P(("stream", "azim"), None, None),
            P("stream", "azim", None),
        ),
        check_vma=False,
    )
```

time: 525 us -> 159 us (0.30); the launches traced: 517 us -> 158 us
  matrix products: 230 us -> 0 us
  other arithmetic: 189 us -> 0 us
  Pallas kernels: 0 us -> 95.3 us
  local copies, waits for them, and re-layouts: 53.6 us -> 16 us
  waiting for transfers between devices: 11.6 us -> 22.5 us
  starting transfers between devices: 29.2 us -> 22.8 us
    dot_general x32 -> x0, matrix products: 230 us -> none  [the longest x16 139 us: advance_group(): jnp.einsum('gbk,gck->gcb', weights, tile_row_count, precision=lax.Precisi...]
    pallas_call x0 -> x4, Pallas kernels: none -> 95.3 us  [the longest x2 85.4 us: bubble_step(): pl.pallas_call(functools.partial(bubble_kernel, first), grid=(1,), out_sh...]
    reduce_sum x32 -> x0, other arithmetic: 75.5 us -> none  [kernel_weights(): return raw / jnp.sum(raw, axis=-1, keepdims=True)]
    scatter-add x2 -> x0, other arithmetic: 48.8 us -> none  [local_update(): jnp.zeros_like(selected).at[:, tile_indices]]
    mul x51 -> x0, other arithmetic: 35.8 us -> none  [the longest x2 28.8 us: fluid_update(): d_azim = 0.5 * (azim_up - azim_down)]
    ppermute x8, waiting for transfers between devices: 11.6 us -> 22.5 us  [the longest x2 21.2 us: exchange(): lax.ppermute(last_col, 'azim', right)]
    add x18 -> x0, other arithmetic: 10.5 us -> none  [the longest x2 9.64 us: fluid_update(): return flow_field + TIME_STEP * change + DIFFUSION * laplace]
    gather x4 -> x0, local copies, waits for them, and re-layouts: 10.4 us -> none  [the longest x2 4.36 us: local_update(): tile_row_count = jnp.take(selected, tile_indices, axis=1).transpose(1, 0, 2)]
  transfers between devices with their start and end apart: 10 -> 9, of which waited for: 2 -> 3; matrix products, arithmetic and copies ran while one was open for 48% -> 2% of each run, Pallas kernels for 0% -> 30%
where the time goes in v1:
time: 159 us; the launch traced here: 158 us
  Pallas kernels  95.3 us (60%)
  starting transfers between devices  22.8 us (14%)
  waiting for transfers between devices  22.5 us (14%)
  local copies, waits for them, and re-layouts  16 us (10%)
    pallas_call x2, Pallas kernels, bubble_step(): pl.pallas_call(functools.partial(bubble_kernel, first), grid=(1,), out_sh...  85.4 us
    ppermute x2, waiting for transfers between devices, exchange(): lax.ppermute(last_col, 'azim', right)  21.2 us
    unnamed x16, local copies, waits for them, and re-layouts  13.3 us
    pallas_call x2, Pallas kernels, fluid_step(): pl.pallas_call(functools.partial(fluid_kernel, edges), grid=(steps,), out...  9.93 us
    all_to_all x1, starting transfers between devices, on_device(): lax.all_to_all(sent, axes, split_axis=0, concat_axis=0, tiled=True)  6.21 us
    ppermute x2, starting transfers between devices, exchange(): lax.ppermute(fluid[:, length - 1:], 'stream', up)  5.99 us
    ppermute x2, starting transfers between devices, exchange(): lax.ppermute(fluid[:, :1], 'stream', down)  5.77 us
    ppermute x2, starting transfers between devices, exchange(): lax.ppermute(first_col, 'azim', left)  3.53 us
  transfers between devices with their start and end apart: 9, of which 3 were waited for; matrix products, arithmetic and copies ran while one was open for 2% of the time, Pallas kernels for 30%

profile of v1, /device:TPU:17, one launch (start us, length us, event | category | flops | bytes accessed | tf_op | source)
XLA Modules:
  0.0 158.0 jit_solution(16498232930439344253)
XLA Ops:
  1.3 2.1 %copy.11.refs_3_ = f32[512,5,128]{2,1,0:T(8,128)S(1)} copy(f32[512,5,128]{2,0,1:T(8,128)} %param.7) | data formatting | bytes 2621440 | tf_op args[1]
  3.4 0.0 copy-start
  3.4 2.2 %copy-done = f32[4,64,32,128]{3,2,1,0:T(8,128)S(1)} copy-done((f32[4,64,32,128]{3,2,1,0:T(8,128)S(1)}, f32[4,64,32,128]{3,2,1,0:T(8,128)}, u32[]{:S(2)}) %copy-start) | copy-done | bytes 4194328
  5.6 0.0 copy-start.4
  5.6 0.7 copy-done.4
  6.3 0.0 copy-start.5
  6.3 0.7 copy-done.5
  7.0 43.1 %bubbles_first.1 = (f32[2560,128]{1,0:T(8,128)}, f32[2048,128]{1,0:T(8,128)S(1)}) custom-call(s32[512]{0:T(512)S(1)} %copy-done.4, s32[512]{0:T(512)S(1)} %copy-done.5, s32[1]{0:T(128)S(6)} %copy.15.refs_2_, f32[512,5,128]{2,1,0:T(8,128)S(1)} %copy.11.refs_3_, f32[4,2048,128]{2,1,0:T(8,128)S(1)} %bitcast.13, f32[4,2048,128]{2,1,0:T(8,128)S(1)} %bitcast.14), custom_call_target="tpu_custom_call" | custom-call | flops 335544320 | bytes 12582912 | tf_op jit(solution)/shard_map/bubbles_first/pallas_call | solution.py:195
  50.0 6.2 %all-to-all-start = ((f32[32,80,128]{2,1,0:T(8,128)}), f32[32,80,128]{2,1,0:T(8,128)S(1)}, u32[]{:S(2)}, u32[]{:S(2)}) async-start(f32[32,80,128]{2,1,0:T(8,128)} %bitcast.4), calls=%async_computation | async-start | bytes 2621440 | tf_op jit(solution)/shard_map/all_to_all | solution.py:329
  56.3 1.7 %fusion.1 = (f32[4,64,1,128]{3,2,1,0:T(1,128)S(1)}, f32[4,64,1,128]{3,2,1,0:T(1,128)S(1)}) fusion(f32[4,64,32,128]{3,2,1,0:T(8,128)} %after_ref.1), kind=kLoop, calls=%fused_computation.1 | loop fusion | bytes 524288 | tf_op jit(solution)/shard_map/slice | solution.py:322
  58.0 1.2 collective-permute-start.2
  59.2 1.2 collective-permute-start.3
  60.4 0.9 fusion.2
  61.3 2.9 %collective-permute-start.1 = (f32[4,1,32,128]{3,2,1,0:T(8,128)S(1)}, f32[4,1,32,128]{3,2,1,0:T(8,128)S(1)}, u32[]{:S(2)}, u32[]{:S(2)}) collective-permute-start(f32[4,1,32,128]{3,2,1,0:T(8,128)S(1)} %get-tuple-element.26), channel_id=1, source_target_pairs={{8,0},{16,8},{24,16},{9,1},{17,9},{25,17},{10,2},{18,10},{26,18},{... | collective-permute-start | bytes 196616 | tf_op jit(solution)/shard_map/ppermute | solution.py:309
  64.2 3.0 %collective-permute-start = (f32[4,1,32,128]{3,2,1,0:T(8,128)S(1)}, f32[4,1,32,128]{3,2,1,0:T(8,128)S(1)}, u32[]{:S(2)}, u32[]{:S(2)}) collective-permute-start(f32[4,1,32,128]{3,2,1,0:T(8,128)S(1)} %get-tuple-element.27), channel_id=1, source_target_pairs={{0,8},{8,16},{16,24},{1,9},{9,17},{17,25},{2,10},{10,18},{18,26},{... | collective-permute-start | bytes 196616 | tf_op jit(solution)/shard_map/ppermute | solution.py:308
  67.2 0.6 collective-permute-done.1.high_ref
  67.8 0.7 collective-permute-done.low_ref
  68.5 21.2 %collective-permute-done.2.left_ref = f32[4,64,128]{2,1,0:T(8,128)S(1)} collective-permute-done((f32[4,64,128]{2,1,0:T(8,128)S(1)}, f32[4,64,128]{2,1,0:T(8,128)S(1)}, u32[]{:S(2)}, u32[]{:S(2)}) %collective-permute-start.2) | collective-permute-done | bytes 131104 | tf_op jit(solution)/shard_map/ppermute | solution.py:310
  89.7 0.0 collective-permute-done.3.right_ref
  89.7 0.0 copy-start.1
  89.7 2.2 %copy-done.1 = f32[4,64,32,128]{3,2,1,0:T(8,128)S(1)} copy-done((f32[4,64,32,128]{3,2,1,0:T(8,128)S(1)}, f32[4,64,32,128]{3,2,1,0:T(8,128)}, u32[]{:S(2)}) %copy-start.1) | copy-done | bytes 4194328
  91.9 0.0 copy-start.6
  91.9 4.3 %fluid_first.1 = (f32[4,64,32,128]{3,2,1,0:T(8,128)S(1)}, f32[4,64,128]{2,1,0:T(8,128)S(1)}, f32[4,64,128]{2,1,0:T(8,128)S(1)}) custom-call(f32[4,64,32,128]{3,2,1,0:T(8,128)S(1)} %copy-done.1, f32[4,64,32,128]{3,2,1,0:T(8,128)S(1)} %copy-done.1, f32[4,64,32,128]{3,2,1,0:T(8,128)S(1)} %copy-done.1, f32[4,1,32,128]{3,2,1,0:T(8,128)S(1)} %collective-permute-done.low_ref, ...), custom_call_target="tpu_custom_call" | custom-call | flops 31457280 | bytes 10485760 | tf_op jit(solution)/shard_map/fluid_first/pallas_call | solution.py:277
  96.2 0.1 collective-permute-start.6
  96.2 2.4 %collective-permute-start.7 = (f32[4,64,128]{2,1,0:T(8,128)S(1)}, f32[4,64,128]{2,1,0:T(8,128)S(1)}, u32[]{:S(2)}, u32[]{:S(2)}) collective-permute-start(f32[4,64,128]{2,1,0:T(8,128)S(1)} %get-tuple-element.14), channel_id=1, source_target_pairs={{1,0},{2,1},{3,2},{4,3},{5,4},{6,5},{7,6},{0,7},{9,8},{10,9},{11,1... | collective-permute-start | bytes 393224 | tf_op jit(solution)/shard_map/ppermute | solution.py:311
  98.6 0.0 copy-start.2
  98.6 2.0 %copy-done.2 = f32[4,64,32,128]{3,2,1,0:T(8,128)} copy-done((f32[4,64,32,128]{3,2,1,0:T(8,128)}, f32[4,64,32,128]{3,2,1,0:T(8,128)S(1)}, u32[]{:S(2)}) %copy-start.2) | copy-done | bytes 4194328
  100.6 2.9 %collective-permute-start.5 = (f32[4,1,32,128]{3,2,1,0:T(8,128)S(1)}, f32[4,1,32,128]{3,2,1,0:T(8,128)S(1)}, u32[]{:S(2)}, u32[]{:S(2)}) collective-permute-start(f32[4,1,32,128]{3,2,1,0:T(8,128)S(1)} %get-tuple-element.22), channel_id=1, source_target_pairs={{8,0},{16,8},{24,16},{9,1},{17,9},{25,17},{10,2},{18,10},{26,18},{... | collective-permute-start | bytes 196616 | tf_op jit(solution)/shard_map/ppermute | solution.py:309
  103.5 3.0 %collective-permute-start.4 = (f32[4,1,32,128]{3,2,1,0:T(8,128)S(1)}, f32[4,1,32,128]{3,2,1,0:T(8,128)S(1)}, u32[]{:S(2)}, u32[]{:S(2)}) collective-permute-start(f32[4,1,32,128]{3,2,1,0:T(8,128)S(1)} %get-tuple-element.23), channel_id=1, source_target_pairs={{0,8},{8,16},{16,24},{1,9},{9,17},{17,25},{2,10},{10,18},{18,26},{... | collective-permute-start | bytes 196616 | tf_op jit(solution)/shard_map/ppermute | solution.py:308
  106.5 0.0 all-to-all-done
  106.6 0.0 copy-done.6
  106.6 0.0 copy-start.3
  106.6 2.2 %copy-done.3 = f32[4,64,32,128]{3,2,1,0:T(8,128)S(1)} copy-done((f32[4,64,32,128]{3,2,1,0:T(8,128)S(1)}, f32[4,64,32,128]{3,2,1,0:T(8,128)}, u32[]{:S(2)}) %copy-start.3) | copy-done | bytes 4194328
  108.8 42.3 %bubbles_second.1 = (f32[512,5,128]{2,1,0:T(8,128)S(1)}, f32[2048,128]{1,0:T(8,128)S(1)}, f32[2048,128]{1,0:T(8,128)}) custom-call(s32[512]{0:T(512)S(1)} %copy-done.6, f32[2560,128]{1,0:T(8,128)S(1)} %bitcast.17, f32[4,2048,128]{2,1,0:T(8,128)S(1)} %bitcast.15, f32[4,2048,128]{2,1,0:T(8,128)S(1)} %bitcast.16), custom_call_target="tpu_custom_call" | custom-call | flops 335544320 | bytes 12582912 | tf_op jit(solution)/shard_map/bubbles_second/pallas_call | solution.py:195
  151.1 1.3 copy.12
  152.3 0.0 collective-permute-done.5.high_ref
  152.3 0.0 collective-permute-done.4.low_ref
  152.4 0.0 collective-permute-done.6.left_ref
  152.4 0.0 collective-permute-done.7.right_ref
  152.4 5.6 %fluid_second.1 = f32[4,64,32,128]{3,2,1,0:T(8,128)} custom-call(f32[4,64,32,128]{3,2,1,0:T(8,128)S(1)} %copy-done.3, f32[4,64,32,128]{3,2,1,0:T(8,128)S(1)} %copy-done.3, f32[4,64,32,128]{3,2,1,0:T(8,128)S(1)} %copy-done.3, f32[4,1,32,128]{3,2,1,0:T(8,128)S(1)} %collective-permute-done.4.low_ref, f32[4,1,32,128]{3,2,1,0:T(8,128)S(1)} %collective-permute-done.5.high_ref, ...), custom_call_target="tpu_custom_call" | custom-call | flops 31457280 | bytes 10485760 | tf_op jit(solution)/shard_map/fluid_second/pallas_call | solution.py:277
  (1 shorter events, 0.0 us)
Async XLA Ops:
  3.4 2.2 %copy-start = (f32[4,64,32,128]{3,2,1,0:T(8,128)S(1)}, f32[4,64,32,128]{3,2,1,0:T(8,128)}, u32[]{:S(2)}) copy-start(f32[4,64,32,128]{3,2,1,0:T(8,128)} %after_ref.1) | copy-start | bytes 12582916
  5.6 0.7 copy-start.4
  6.3 0.7 copy-start.5
  50.0 56.5 %all-to-all-start = ((f32[32,80,128]{2,1,0:T(8,128)}), f32[32,80,128]{2,1,0:T(8,128)S(1)}, u32[]{:S(2)}, u32[]{:S(2)}) async-start(f32[32,80,128]{2,1,0:T(8,128)} %bitcast.4), calls=%async_computation | async-start | bytes 2621440 | tf_op jit(solution)/shard_map/all_to_all | solution.py:329
  58.0 31.7 %collective-permute-start.2 = (f32[4,64,128]{2,1,0:T(8,128)S(1)}, f32[4,64,128]{2,1,0:T(8,128)S(1)}, u32[]{:S(2)}, u32[]{:S(2)}) collective-permute-start(f32[4,64,128]{2,1,0:T(8,128)S(1)} %bitcast.21), channel_id=1, source_target_pairs={{0,1},{1,2},{2,3},{3,4},{4,5},{5,6},{6,7},{7,0},{8,9},{9,10},{10,1... | collective-permute-start | bytes 393224 | tf_op jit(solution)/shard_map/ppermute | solution.py:310
  59.2 30.4 %collective-permute-start.3 = (f32[4,64,128]{2,1,0:T(8,128)S(1)}, f32[4,64,128]{2,1,0:T(8,128)S(1)}, u32[]{:S(2)}, u32[]{:S(2)}) collective-permute-start(f32[4,64,128]{2,1,0:T(8,128)S(1)} %bitcast.20), channel_id=1, source_target_pairs={{1,0},{2,1},{3,2},{4,3},{5,4},{6,5},{7,6},{0,7},{9,8},{10,9},{11,1... | collective-permute-start | bytes 393224 | tf_op jit(solution)/shard_map/ppermute | solution.py:311
  61.3 6.5 %collective-permute-start.1 = (f32[4,1,32,128]{3,2,1,0:T(8,128)S(1)}, f32[4,1,32,128]{3,2,1,0:T(8,128)S(1)}, u32[]{:S(2)}, u32[]{:S(2)}) collective-permute-start(f32[4,1,32,128]{3,2,1,0:T(8,128)S(1)} %get-tuple-element.26), channel_id=1, source_target_pairs={{8,0},{16,8},{24,16},{9,1},{17,9},{25,17},{10,2},{18,10},{26,18},{... | collective-permute-start | bytes 196616 | tf_op jit(solution)/shard_map/ppermute | solution.py:309
  64.2 4.3 %collective-permute-start = (f32[4,1,32,128]{3,2,1,0:T(8,128)S(1)}, f32[4,1,32,128]{3,2,1,0:T(8,128)S(1)}, u32[]{:S(2)}, u32[]{:S(2)}) collective-permute-start(f32[4,1,32,128]{3,2,1,0:T(8,128)S(1)} %get-tuple-element.27), channel_id=1, source_target_pairs={{0,8},{8,16},{16,24},{1,9},{9,17},{17,25},{2,10},{10,18},{18,26},{... | collective-permute-start | bytes 196616 | tf_op jit(solution)/shard_map/ppermute | solution.py:308
  89.7 2.2 %copy-start.1 = (f32[4,64,32,128]{3,2,1,0:T(8,128)S(1)}, f32[4,64,32,128]{3,2,1,0:T(8,128)}, u32[]{:S(2)}) copy-start(f32[4,64,32,128]{3,2,1,0:T(8,128)} %after_ref.1) | copy-start | bytes 12582916
  91.9 14.7 %copy-start.6 = (s32[512]{0:T(512)S(1)}, s32[512]{0:T(512)}, u32[]{:S(2)}) copy-start(s32[512]{0:T(512)} %refs_0_.3) | copy-start | bytes 6148
  96.2 56.2 %collective-permute-start.6 = (f32[4,64,128]{2,1,0:T(8,128)S(1)}, f32[4,64,128]{2,1,0:T(8,128)S(1)}, u32[]{:S(2)}, u32[]{:S(2)}) collective-permute-start(f32[4,64,128]{2,1,0:T(8,128)S(1)} %get-tuple-element.13), channel_id=1, source_target_pairs={{0,1},{1,2},{2,3},{3,4},{4,5},{5,6},{6,7},{7,0},{8,9},{9,10},{10,1... | collective-permute-start | bytes 393224 | tf_op jit(solution)/shard_map/ppermute | solution.py:310
  96.2 56.1 %collective-permute-start.7 = (f32[4,64,128]{2,1,0:T(8,128)S(1)}, f32[4,64,128]{2,1,0:T(8,128)S(1)}, u32[]{:S(2)}, u32[]{:S(2)}) collective-permute-start(f32[4,64,128]{2,1,0:T(8,128)S(1)} %get-tuple-element.14), channel_id=1, source_target_pairs={{1,0},{2,1},{3,2},{4,3},{5,4},{6,5},{7,6},{0,7},{9,8},{10,9},{11,1... | collective-permute-start | bytes 393224 | tf_op jit(solution)/shard_map/ppermute | solution.py:311
  98.6 2.0 %copy-start.2 = (f32[4,64,32,128]{3,2,1,0:T(8,128)}, f32[4,64,32,128]{3,2,1,0:T(8,128)S(1)}, u32[]{:S(2)}) copy-start(f32[4,64,32,128]{3,2,1,0:T(8,128)S(1)} %get-tuple-element.12.f_ref.before_ref.after_ref) | copy-start | bytes 12582916
  100.6 51.7 %collective-permute-start.5 = (f32[4,1,32,128]{3,2,1,0:T(8,128)S(1)}, f32[4,1,32,128]{3,2,1,0:T(8,128)S(1)}, u32[]{:S(2)}, u32[]{:S(2)}) collective-permute-start(f32[4,1,32,128]{3,2,1,0:T(8,128)S(1)} %get-tuple-element.22), channel_id=1, source_target_pairs={{8,0},{16,8},{24,16},{9,1},{17,9},{25,17},{10,2},{18,10},{26,18},{... | collective-permute-start | bytes 196616 | tf_op jit(solution)/shard_map/ppermute | solution.py:309
  103.5 48.8 %collective-permute-start.4 = (f32[4,1,32,128]{3,2,1,0:T(8,128)S(1)}, f32[4,1,32,128]{3,2,1,0:T(8,128)S(1)}, u32[]{:S(2)}, u32[]{:S(2)}) collective-permute-start(f32[4,1,32,128]{3,2,1,0:T(8,128)S(1)} %get-tuple-element.23), channel_id=1, source_target_pairs={{0,8},{8,16},{16,24},{1,9},{9,17},{17,25},{2,10},{10,18},{18,26},{... | collective-permute-start | bytes 196616 | tf_op jit(solution)/shard_map/ppermute | solution.py:308
  106.6 2.2 %copy-start.3 = (f32[4,64,32,128]{3,2,1,0:T(8,128)S(1)}, f32[4,64,32,128]{3,2,1,0:T(8,128)}, u32[]{:S(2)}) copy-start(f32[4,64,32,128]{3,2,1,0:T(8,128)} %copy-done.2) | copy-start | bytes 12582916
